TPU v7x, 256 devices: a whole 4x4x8 slice. The times are simulated.
256 devices in a mesh: tok: 16 (over z_lo, y, core), head: 16 (over x, z_hi).
Axes of the slice: x: 4, y: 4, z: 8 (z_hi: 4, z_lo: 2; z = z_hi * 2 + z_lo), core: 2. Of those that a mesh axis runs over, the one named last changes fastest.
Arguments:
- tokens: bfloat16 [8192, 4096], P('tok', 'head'), may hold values from -32 to 32
- w_query: bfloat16 [4096, 4096], P(None, 'head'), may hold values from -0.09375 to 0.09375
- w_key: bfloat16 [4096, 4096], P(None, 'head'), may hold values from -0.09375 to 0.09375
- w_value: bfloat16 [4096, 4096], P(None, 'head'), may hold values from -0.09375 to 0.09375
- w_out: bfloat16 [4096, 4096], P('head'), may hold values from -0.09375 to 0.09375
- fast_gate: float32 [32, 128, 256], P('head'), may hold values from -0.5 to 0.5
- fast_up: float32 [32, 128, 256], P('head'), may hold values from -0.5 to 0.5
- fast_down: float32 [32, 256, 128], P('head'), may hold values from -0.375 to 0.375
- token_rate: float32 [8192, 32], P('tok', 'head'), may hold values from 0.05 to 1
- head_step: float32 [32], P('head'), may hold values from 0.2 to 1
Outputs:
- mixed: bfloat16 [8192, 4096], P(('tok', 'head'))
All inputs are finite; a program needn't handle non-finite values.
Results may differ from a plain program's by a relative error of at most 0.022.
Values may be sent and summed in bfloat16 or wider, within the bound.
A program may use at most 64 MiB of HBM per device.

v0:
```python
import jax
import jax.numpy as jnp
from jax import lax
from jax.sharding import PartitionSpec as P

WINDOW = 512


def shifted(value, axis, steps):
    count = lax.axis_size(axis)
    leading, last = (max(0, -steps), min(count, count - steps))
    return lax.ppermute(value, axis, [(source, source + steps) for source in range(leading, last)])


def rms(values):
    return values * lax.rsqrt(jnp.mean(values * values, axis=-1, keepdims=True) + 1e-06)


def batched(form, left, right):
    return jnp.einsum(form, left, right, precision=lax.Precision.HIGHEST)


def fast_apply(inputs, gate, upper, down):
    gate_pre = batched("thd,hdf->thf", inputs, gate)
    up_pre = batched("thd,hdf->thf", inputs, upper)
    return batched("thf,hfd->thd", jax.nn.silu(gate_pre) * up_pre, down)


def shards(
    tokens, w_query, w_key, w_value, w_out, fast_gate, fast_up, fast_down, token_rate, head_step
):
    row_count = tokens.shape[0]
    local_heads = fast_gate.shape[0]
    head_size = fast_gate.shape[1]
    hidden_size = fast_gate.shape[2]
    local_width = local_heads * head_size
    piece = lax.all_gather(tokens, "head", axis=1, tiled=True)
    query_f, key_f, value_f = tuple(
        (
            jnp.dot(piece, weight, preferred_element_type=jnp.float32)
            for weight in (w_query, w_key, w_value)
        )
    )
    shape = (row_count, local_heads, head_size)
    query = query_f.astype(jnp.bfloat16).reshape(shape)
    key = key_f.astype(jnp.bfloat16).reshape(shape)
    value = value_f.astype(jnp.bfloat16).reshape(shape)
    window = WINDOW
    tail = jnp.stack([key, value])
    before = shifted(tail, "tok", 1)
    keys_all = jnp.concatenate([before[0], key], axis=0)
    values_all = jnp.concatenate([before[1], value], axis=0)
    first = lax.axis_index("tok") * row_count
    query_pos = first + jnp.arange(row_count, dtype=jnp.int32)
    key_pos = first - window + jnp.arange(row_count + window, dtype=jnp.int32)
    allowed = (
        (key_pos[None, :] >= 0)
        & (key_pos[None, :] <= query_pos[:, None])
        & (key_pos[None, :] > query_pos[:, None] - window)
    )
    scores = jnp.einsum(
        "qhd,khd->hqk", query, keys_all, preferred_element_type=jnp.float32
    ) * head_size ** (-0.5)
    scores = jnp.where(allowed[None], scores, jnp.float32(-1e30))
    top = jnp.max(scores, axis=-1, keepdims=True)
    expo = jnp.exp(scores - top)
    weights = (expo / jnp.sum(expo, axis=-1, keepdims=True)).astype(jnp.bfloat16)
    attended = jnp.einsum("hqk,khd->qhd", weights, values_all, preferred_element_type=jnp.float32)
    knorm = rms(key.astype(jnp.float32))
    qnorm = rms(query.astype(jnp.float32))
    target = -token_rate[:, :, None] * value.astype(jnp.float32)
    gate_pre = batched("thd,hdf->thf", knorm, fast_gate)
    up_pre = batched("thd,hdf->thf", knorm, fast_up)
    sigma = jax.nn.sigmoid(gate_pre)
    active = gate_pre * sigma
    hidden = active * up_pre
    grad_down_t = batched("thf,thd->hdf", hidden, target)
    back = batched("thd,hfd->thf", target, fast_down)
    grad_up = batched("thd,thf->hdf", knorm, back * active)
    grad_gate = batched(
        "thd,thf->hdf", knorm, back * up_pre * sigma * (1.0 + gate_pre * (1.0 - sigma))
    )
    grads = jnp.stack([grad_gate, grad_up, grad_down_t], axis=1)
    matrices = jnp.stack([fast_gate, fast_up, jnp.transpose(fast_down, (0, 2, 1))], axis=1)
    fan_scale = jnp.array(
        [head_size ** (-0.5), head_size ** (-0.5), hidden_size ** (-0.5)], jnp.float32
    )
    step_scale = head_step[:, None, None, None] * fan_scale[None, :, None, None]
    count = head_size * hidden_size
    summed = lax.psum(grads.astype(jnp.bfloat16), "tok").astype(jnp.float32)
    mean_sq = jnp.sum(summed * summed, axis=(2, 3)) / count
    renewed = matrices - step_scale * summed * lax.rsqrt(mean_sq + 1e-06)[:, :, None, None]
    fast_out = fast_apply(
        qnorm, renewed[:, 0], renewed[:, 1], jnp.transpose(renewed[:, 2], (0, 2, 1))
    )
    combined = (attended + fast_out).astype(jnp.bfloat16).reshape(row_count, local_width)
    return lax.psum_scatter(
        jnp.dot(combined, w_out, preferred_element_type=jnp.float32).astype(jnp.bfloat16),
        "head",
        scatter_dimension=0,
        tiled=True,
    )


def solution(mesh):
    placed = (
        P("tok", "head"),
        P(None, "head"),
        P(None, "head"),
        P(None, "head"),
        P("head", None),
        P("head", None, None),
        P("head", None, None),
        P("head", None, None),
        P("tok", "head"),
        P("head"),
    )
    return jax.shard_map(
        shards, mesh=mesh, in_specs=placed, out_specs=P(("tok", "head"), None), check_vma=False
    )
```

profile of v0, /device:TPU:1, one launch (start us, length us, event | category | flops | bytes accessed | tf_op | source)
XLA Modules:
  0.0 348.3 jit_solution(3736179708605221274)
XLA Ops:
  6.5 0.0 copy-start
  6.5 0.0 all-gather.2.cloned.1.call-start
  6.5 0.7 all-gather.2.cloned.1.call-update
  7.3 0.0 all-reduce.2.cloned.1.call-start
  7.3 0.7 neg.11
  8.0 1.1 copy.18
  9.1 0.7 broadcast_multiply_fusion
  9.9 1.4 compare_and_fusion
  11.3 0.0 copy-start.2
  11.3 0.0 copy-start.1
  11.3 83.8 %all-gather.2.cloned.1.call-done = bf16[512,4096]{1,0:T(8,128)(2,1)} async-done(((bf16[512,256]{1,0:T(8,128)(2,1)}), bf16[512,4096]{1,0:T(8,128)(2,1)}) %all-gather.2.cloned.1.call-update) | async-done | bytes 4194320 | tf_op jit(solution)/shard_map/all_gather | solution.py:37
  95.1 0.0 copy-start.8
  95.1 0.0 copy-start.9
  95.1 4.3 %fusion.24 = (f32[512,2]{0,1:T(2,128)S(1)}, bf16[512,256]{0,1:T(8,128)(2,1)S(1)}) fusion(bf16[512,4096]{1,0:T(8,128)(2,1)} %all-gather.2.cloned.1.call-done, bf16[4096,256]{1,0:T(8,128)(2,1)} %param.13), kind=kOutput, calls=%fused_computation.47 | convolution fusion | flops 1074265088 | bytes 6557696 | tf_op jit(solution)/shard_map/dot_general | solution.py:40
  99.4 0.0 copy-done.2
  99.4 1.0 convolution_bitcast_fusion.2
  100.4 0.0 copy-done.1
  100.5 1.0 convolution_bitcast_fusion.3
  101.5 0.0 copy-done.8
  101.5 0.0 copy-done.9
  101.5 0.0 copy-start.3
  101.5 1.3 convolution_convert_fusion.2
  102.8 0.0 copy-done.3
  102.8 1.0 convolution_bitcast_fusion.4
  103.9 1.1 fusion.11
  104.9 1.2 fusion.9
  106.1 1.1 fusion.10
  107.2 0.8 copy.13
  108.0 0.9 copy.12
  108.9 0.8 pad_maximum_fusion.1
  109.7 0.0 all-reduce.2.cloned.1.call-update
  109.7 0.0 reduce-scatter.2.cloned.1.call-start
  109.7 0.0 copy-start.4
  109.8 0.0 copy-start.5
  109.8 4.2 %convolution_convert_fusion.1 = bf16[512,256]{0,1:T(8,128)(2,1)S(1)} fusion(bf16[512,4096]{1,0:T(8,128)(2,1)} %all-gather.2.cloned.1.call-done, bf16[4096,256]{1,0:T(8,128)(2,1)} %param.12), kind=kOutput, calls=%fused_computation.19 | convolution fusion | flops 1073872896 | bytes 6553600 | tf_op jit(solution)/shard_map/dot_general | solution.py:40
  114.0 0.0 copy-done.4
  114.0 0.0 copy-done.5
  114.0 0.8 pad_maximum_fusion
  114.8 0.8 copy.14
  115.7 0.2 copy.15
  115.9 0.2 copy.22
  116.0 4.3 %collective-permute-start = (bf16[2,512,2,128]{3,1,2,0:T(8,128)(2,1)}, bf16[2,512,2,128]{3,1,2,0:T(8,128)(2,1)}, u32[]{:S(2)}, u32[]{:S(2)}) collective-permute-start(bf16[2,512,2,128]{3,1,2,0:T(8,128)(2,1)} %pad_maximum_fusion), channel_id=1, source_target_pairs={{0,16},{16,32},{32,48},{48,64},{64,80},{80,96},{96,112},{112,128},... | collective-permute-start | bytes 1572872 | tf_op jit(solution)/shard_map/ppermute | solution.py:12
  120.3 0.2 fusion.25
  120.6 110.9 %all-reduce.2.cloned.1.call-done = bf16[2,3,128,256]{3,2,0,1:T(8,128)(2,1)} async-done(((bf16[2,3,128,256]{3,2,0,1:T(8,128)(2,1)}), bf16[2,3,128,256]{3,2,0,1:T(8,128)(2,1)}) %all-reduce.2.cloned.1.call-update) | async-done | bytes 393232 | tf_op jit(solution)/shard_map/psum | solution.py:90
  231.4 1.2 fusion.23
  232.6 1.2 fusion.22
  233.9 1.0 convolution_bitcast_fusion.1
  234.9 1.2 fusion.6
  236.1 0.0 copy-start.6
  236.1 1.2 fusion.34
  237.3 0.0 collective-permute-done
  237.3 1.1 slice_bitcast_fusion.7
  238.4 0.8 fusion.29
  239.1 0.0 copy-done.6
  239.1 0.0 copy-start.7
  239.1 2.0 fusion.52
  241.2 0.0 copy-done.7
  241.2 1.0 fusion.8
  242.1 0.0 copy-done
  242.2 3.2 convolution_convert_fusion
  245.4 0.0 reduce-scatter.2.cloned.1.call-update
  245.4 96.4 %reduce-scatter.2.cloned.1.call-done = bf16[32,4096]{1,0:T(8,128)(2,1)} async-done(((bf16[512,4096]{1,0:T(8,128)(2,1)}), bf16[32,4096]{1,0:T(8,128)(2,1)}) %reduce-scatter.2.cloned.1.call-update) | async-done | bytes 262160 | tf_op jit(solution)/shard_map/reduce_scatter | solution.py:97
  (6 shorter events, 0.0 us)
Async XLA Ops:
  6.5 235.6 %copy-start = (bf16[256,4096]{1,0:T(8,128)(2,1)S(1)}, bf16[256,4096]{1,0:T(8,128)(2,1)}, u32[]{:S(2)}) copy-start(bf16[256,4096]{1,0:T(8,128)(2,1)} %param.15) | copy-start | bytes 6291460
  6.5 88.5 %all-gather.2.cloned.1.call-start = ((), (), s32[]{:S(2)}) async-start(), calls=%async_computation.1 | async-start | bytes 4456448 | tf_op jit(solution)/shard_map/all_gather | solution.py:37
  7.3 224.2 %all-reduce.2.cloned.1.call-start = ((), (), s32[]{:S(2)}) async-start(), calls=%async_computation.2 | async-start | bytes 786432 | tf_op jit(solution)/shard_map/psum | solution.py:90
  11.3 88.1 %copy-start.2 = (f32[2,128,256]{2,1,0:T(8,128)S(1)}, f32[2,128,256]{2,1,0:T(8,128)}, u32[]{:S(2)}) copy-start(f32[2,128,256]{2,1,0:T(8,128)} %param.16) | copy-start | bytes 786436
  11.3 89.2 %copy-start.1 = (f32[2,128,256]{2,1,0:T(8,128)S(1)}, f32[2,128,256]{2,1,0:T(8,128)}, u32[]{:S(2)}) copy-start(f32[2,128,256]{2,1,0:T(8,128)} %param.17) | copy-start | bytes 786436
  95.1 6.4 %copy-start.8 = (bf16[512,4096]{1,0:T(8,128)(2,1)S(1)}, bf16[512,4096]{1,0:T(8,128)(2,1)}, u32[]{:S(2)}) copy-start(bf16[512,4096]{1,0:T(8,128)(2,1)} %all-gather.2.cloned.1.call-done) | copy-start | bytes 12582916
  95.1 6.4 %copy-start.9 = (bf16[4096,256]{1,0:T(8,128)(2,1)S(1)}, bf16[4096,256]{1,0:T(8,128)(2,1)}, u32[]{:S(2)}) copy-start(bf16[4096,256]{1,0:T(8,128)(2,1)} %param.14) | copy-start | bytes 6291460
  101.5 1.3 copy-start.3
  109.7 232.1 %reduce-scatter.2.cloned.1.call-start = ((), (), s32[]{:S(2)}) async-start(), calls=%async_computation.3 | async-start | bytes 4456448 | tf_op jit(solution)/shard_map/reduce_scatter | solution.py:97
  109.7 4.2 %copy-start.4 = (bf16[1,512,2,128]{3,1,2,0:T(8,128)(2,1)S(1)}, bf16[1,512,2,128]{3,1,2,0:T(8,128)(2,1)}, u32[]{:S(2)}) copy-start(bf16[1,512,2,128]{3,1,2,0:T(8,128)(2,1)} %copy.13) | copy-start | bytes 786436
  109.8 4.2 %copy-start.5 = (bf16[1,512,2,128]{3,1,2,0:T(8,128)(2,1)S(1)}, bf16[1,512,2,128]{3,1,2,0:T(8,128)(2,1)}, u32[]{:S(2)}) copy-start(bf16[1,512,2,128]{3,1,2,0:T(8,128)(2,1)} %copy.12) | copy-start | bytes 786436
  116.0 121.2 %collective-permute-start = (bf16[2,512,2,128]{3,1,2,0:T(8,128)(2,1)}, bf16[2,512,2,128]{3,1,2,0:T(8,128)(2,1)}, u32[]{:S(2)}, u32[]{:S(2)}) collective-permute-start(bf16[2,512,2,128]{3,1,2,0:T(8,128)(2,1)} %pad_maximum_fusion), channel_id=1, source_target_pairs={{0,16},{16,32},{32,48},{48,64},{64,80},{80,96},{96,112},{112,128},... | collective-permute-start | bytes 1572872 | tf_op jit(solution)/shard_map/ppermute | solution.py:12
  236.1 3.0 copy-start.6
  239.1 2.1 copy-start.7
Sparse Core Ops, SparseCore 0:
  9.7 85.2 all-gather.1
  109.8 121.5 all-reduce.1
  245.5 96.2 reduce-scatter.1
where the time goes:
time: 349 us; the launch traced here: 348 us
  waiting for transfers between devices  292 us (84%)
  matrix products  24.5 us (7%)
  between operations  13.4 us (4%)
  other arithmetic  9.21 us (3%)
  local copies, waits for them, and re-layouts  5.09 us (1%)
  starting transfers between devices  4.36 us (1%)
    psum x1, waiting for transfers between devices, shards(): summed = lax.psum(grads.astype(jnp.bfloat16), 'tok').astype(jnp.float32)  111 us
    reduce_scatter x1, waiting for transfers between devices, shards(): lax.psum_scatter(jnp.dot(combined, w_out, preferred_element_type=jnp.floa...  96.4 us
    all_gather x1, waiting for transfers between devices, shards(): piece = lax.all_gather(tokens, 'head', axis=1, tiled=True)  83.8 us
    dot_general x3, matrix products, shards(): jnp.dot(piece, weight, preferred_element_type=jnp.float32)  9.8 us
    dot_general x9, matrix products, batched(): return jnp.einsum(form, left, right, precision=lax.Precision.HIGHEST)  9.73 us
  transfers between devices with their start and end apart: 4, of which 3 were waited for; matrix products, arithmetic and copies ran while one was open for 5% of the time, Pallas kernels for 0%

commit v1 on v0

v1 whole, which is shorter than its diff:
```python
import functools
import heapq

import jax
import jax.numpy as jnp
from jax import lax
from jax.experimental import pallas as pl
from jax.experimental.pallas import tpu as pltpu
from jax.sharding import PartitionSpec as P

MESH = pl.DeviceIdType.MESH
WINDOW = 512
SIDE = 4
F32 = jnp.float32
BF16 = jnp.bfloat16
MIRRORS = ((1, 1), (-1, 1), (1, -1), (-1, -1))


def tree_of(sx, sz):
    come = {(0, sz % 4): ("z", sz), (0, -sz % 4): ("z", -sz)}
    for b in (0, 1, 3):
        come[(sx % 4, b)] = ("x", sx)
        come[(-sx % 4, b)] = ("x", -sx)
        come[(2, b)] = ("x", sx)
    come[(0, 2)] = ("z", sz)
    come[(-sx % 4, 2)] = ("x", -sx)
    come[(sx % 4, 2)] = ("z", -sz)
    come[(2, 2)] = ("z", sz)
    return come


def from_of(spot, way):
    axis, sign = way
    return ((spot[0] - sign) % 4, spot[1]) if axis == "x" else (spot[0], (spot[1] - sign) % 4)


def below_of(come):
    below = {}
    for spot, way in come.items():
        below.setdefault(from_of(spot, way), []).append(spot)
    return below


def height(below, spot):
    return max([1 + height(below, s) for s in below.get(spot, [])], default=0)


def plan(trees, size):
    rate = {"x": 46.8e3, "z": 23.4e3}
    late = {"x": 1.8, "z": 2.6}
    belows = [below_of(t) for t in trees]
    free = {(a, s): 0.0 for a in "xz" for s in (1, -1)}
    heap, count, order = [], 0, []

    def send(when, piece, spot):
        nonlocal count
        for to in sorted(belows[piece].get(spot, []), key=lambda s: -height(belows[piece], s)):
            way = trees[piece][to]
            begin = max(when, free[way])
            free[way] = begin + size / rate[way[0]]
            count += 1
            heapq.heappush(heap, (free[way] + late[way[0]], count, piece, to))

    for piece in range(len(trees)):
        send(0.0, piece, (0, 0))
    while heap:
        when, _, piece, spot = heapq.heappop(heap)
        order.append((piece, spot))
        send(when, piece, spot)
    return order


def slot(spot):
    return spot[0] * SIDE + spot[1]


def dot(a, b, dims=((1,), (0,))):
    return lax.dot_general(a, b, (dims, ((), ())), preferred_element_type=F32)


def unit(u):
    return u * lax.rsqrt(jnp.mean(u * u, axis=-1, keepdims=True) + 1e-06)


def kernel(
    tok_n, tokens, w_query, w_key, w_value, w_out, gate, upper, down, rate, step,
    out,
    blocks, w_in, w_o, acc, q, kv, g_w, u_w, d_w, kn_s, tg_s, hid_s, dup_s, dgate_s,
    grad, grad_in, grad_sum, att, comb, part, come_in, go_out,
    load_sem, ag_send, ag_recv, halo_send, halo_recv, ar_send, ar_recv, rs_send, rs_recv,
):
    rows = tokens.shape[0]
    width = tokens.shape[1]
    heads, head_size, hidden = g_w.shape
    t = lax.axis_index("tok")
    h = lax.axis_index("head")
    x, z = h // SIDE, lax.rem(h, SIDE)

    def at(way):
        axis, sign = way
        if axis == "x":
            return (t, lax.rem(x + (SIDE + sign), SIDE) * SIDE + z)
        return (t, x * SIDE + lax.rem(z + (SIDE + sign), SIDE))

    def owner(spot):
        a, b = spot
        return lax.rem(x + (SIDE - a), SIDE) * SIDE + lax.rem(z + (SIDE - b), SIDE)

    def tok_at(k):
        return (lax.rem(t + k, tok_n), h)

    loads = [pltpu.make_async_copy(tokens, blocks.at[0], load_sem.at[0])]
    for j, w in enumerate((w_query, w_key, w_value)):
        loads.append(pltpu.make_async_copy(w, w_in.at[j], load_sem.at[1 + j]))
    loads.append(pltpu.make_async_copy(gate, g_w, load_sem.at[4]))
    loads.append(pltpu.make_async_copy(upper, u_w, load_sem.at[5]))
    loads.append(pltpu.make_async_copy(down, d_w, load_sem.at[6]))
    loads.append(pltpu.make_async_copy(w_out, w_o, load_sem.at[7]))
    for c in loads:
        c.start()

    barrier = pltpu.get_barrier_semaphore()
    ways = [("x", 1), ("x", -1), ("z", 1), ("z", -1)]
    for way in ways:
        pl.semaphore_signal(barrier, inc=1, device_id=at(way), device_id_type=MESH)
    for k in range(1, tok_n):
        pl.semaphore_signal(barrier, inc=1, device_id=tok_at(k), device_id_type=MESH)
    pl.semaphore_wait(barrier, len(ways) + tok_n - 1)

    trees = [tree_of(*m) for m in MIRRORS]
    belows = [below_of(tr) for tr in trees]
    piece_rows = rows // len(trees)
    order = plan(trees, piece_rows * width * 2)

    def ag_copy(p, to):
        frm = from_of(to, trees[p][to])
        span = pl.ds(p * piece_rows, piece_rows)
        src = tokens.at[span] if frm == (0, 0) else blocks.at[slot(frm), span]
        k = p * 16 + slot(to)
        return pltpu.make_async_remote_copy(
            src_ref=src, dst_ref=blocks.at[slot(to), span], send_sem=ag_send.at[k], recv_sem=ag_recv.at[k],
            device_id=at(trees[p][to]), device_id_type=MESH,
        )

    def ag_forward(p, spot):
        for to in sorted(belows[p].get(spot, []), key=lambda s: -height(belows[p], s)):
            ag_copy(p, to).start()

    for p in range(len(trees)):
        ag_forward(p, (0, 0))

    def project(spot, first):
        base = pl.multiple_of(owner(spot) * width, width)

        def one(j, carry):
            prod = dot(blocks[slot(spot)], w_in[j, pl.ds(base, width)])
            acc[j] = prod if first else acc[j] + prod
            return carry

        lax.fori_loop(0, 3, one, 0)

    for c in loads[:4]:
        c.wait()
    project((0, 0), True)
    missing = {}
    for p, spot in order:
        ag_copy(p, spot).wait_recv()
        ag_forward(p, spot)
        missing[spot] = missing.get(spot, len(trees)) - 1
        if missing[spot] == 0:
            project(spot, False)

    for i in range(heads):
        cols = slice(i * head_size, (i + 1) * head_size)
        kv[i, pl.ds(WINDOW, rows)] = acc[1, :, cols].astype(BF16)
        kv[heads + i, pl.ds(WINDOW, rows)] = acc[2, :, cols].astype(BF16)
    halo = []
    for i in range(2 * heads):
        halo.append(pltpu.make_async_remote_copy(
            src_ref=kv.at[i, pl.ds(rows, WINDOW)], dst_ref=kv.at[i, pl.ds(0, WINDOW)],
            send_sem=halo_send.at[i], recv_sem=halo_recv.at[i], device_id=tok_at(1), device_id_type=MESH,
        ))
        halo[-1].start()
    for i in range(heads):
        q[i] = acc[0, :, i * head_size:(i + 1) * head_size].astype(BF16)

    for c in loads[4:7]:
        c.wait()
    chunk = 128

    def grads(i, carry):
        gw = g_w[i].astype(BF16)
        uw = u_w[i].astype(BF16)
        dw = d_w[i].astype(BF16)

        def some(r, inner):
            span = pl.ds(pl.multiple_of(r * chunk, chunk), chunk)
            here = pl.ds(pl.multiple_of(r * chunk, chunk) + WINDOW, chunk)
            kn = unit(kv[i, here].astype(F32)).astype(BF16)
            each = rate[span]
            lane = lax.broadcasted_iota(jnp.int32, each.shape, 1)
            mine = jnp.sum(jnp.where(lane == i, each, 0.0), axis=1, keepdims=True)
            tg = (-mine * kv[heads + i, here].astype(F32)).astype(BF16)
            gate_pre = dot(kn, gw)
            up_pre = dot(kn, uw)
            back = dot(tg, dw, ((1,), (1,)))
            sigma = jax.nn.sigmoid(gate_pre)
            active = gate_pre * sigma
            kn_s[span] = kn
            tg_s[span] = tg
            hid_s[span] = (active * up_pre).astype(BF16)
            dup_s[span] = (back * active).astype(BF16)
            dgate_s[span] = (back * up_pre * sigma * (1.0 + gate_pre * (1.0 - sigma))).astype(BF16)
            return inner

        lax.fori_loop(0, rows // chunk, some, 0)
        base = pl.multiple_of(i * (3 * head_size), head_size)
        kn_all = kn_s[...]
        grad[pl.ds(base, head_size)] = dot(kn_all, dgate_s[...], ((0,), (0,))).astype(BF16)
        grad[pl.ds(base + head_size, head_size)] = dot(kn_all, dup_s[...], ((0,), (0,))).astype(BF16)
        grad[pl.ds(base + 2 * head_size, head_size)] = dot(tg_s[...], hid_s[...], ((0,), (0,))).astype(BF16)
        return carry

    lax.fori_loop(0, heads, grads, 0)

    slice_rows = grad.shape[0] // tok_n
    scatter = []
    for k in range(1, tok_n):
        to = lax.rem(t + k, tok_n)
        scatter.append(pltpu.make_async_remote_copy(
            src_ref=grad.at[pl.ds(pl.multiple_of(to * slice_rows, slice_rows), slice_rows)], dst_ref=grad_in.at[k],
            send_sem=ar_send.at[k], recv_sem=ar_recv.at[k], device_id=(to, h), device_id_type=MESH,
        ))
        scatter[-1].start()

    def attend(i):
        keys_n = WINDOW + chunk

        def some(b, carry):
            first = pl.multiple_of(b * chunk, chunk)
            keys = kv[i, pl.ds(first, keys_n)]
            scores = dot(q[i, pl.ds(first, chunk)], keys, ((1,), (1,))) * head_size ** (-0.5)
            r = lax.broadcasted_iota(jnp.int32, scores.shape, 0)
            c = lax.broadcasted_iota(jnp.int32, scores.shape, 1)
            allowed = (c > r) & (c <= r + WINDOW) & (c >= WINDOW - first - t * rows)
            scores = jnp.where(allowed, scores, -1e30)
            top = jnp.max(scores, axis=-1, keepdims=True)
            expo = jnp.exp(scores - top)
            weights = (expo * (1.0 / jnp.sum(expo, axis=-1, keepdims=True))).astype(BF16)
            att[i, pl.ds(first, chunk)] = dot(weights, kv[heads + i, pl.ds(first, keys_n)])
            return carry

        lax.fori_loop(0, rows // chunk, some, 0)

    for c in halo:
        c.wait_recv()
    attend(0)

    mine = pl.ds(pl.multiple_of(t * slice_rows, slice_rows), slice_rows)
    total = grad[mine].astype(F32)
    for k, c in enumerate(scatter, 1):
        c.wait_recv()
        total = total + grad_in[k].astype(F32)
    grad_sum[mine] = total.astype(BF16)
    share = []
    for k in range(1, tok_n):
        share.append(pltpu.make_async_remote_copy(
            src_ref=grad_sum.at[mine], dst_ref=grad_sum.at[mine],
            send_sem=ar_send.at[tok_n + k], recv_sem=ar_recv.at[tok_n + k], device_id=tok_at(k), device_id_type=MESH,
        ))
        share[-1].start()
    for i in range(1, heads):
        attend(i)
    for c in share:
        c.wait_recv()

    def apply(i, carry):
        base = pl.multiple_of(i * (3 * head_size), head_size)

        def renew(j, matrix, fan_in):
            g = grad_sum[pl.ds(base + j * head_size, head_size)].astype(F32)
            mean_sq = jnp.sum(jnp.sum(g * g, axis=1, keepdims=True), axis=0, keepdims=True) / (head_size * hidden)
            return (matrix - (step[i] * fan_in ** (-0.5)) * g * lax.rsqrt(mean_sq + 1e-06)).astype(BF16)

        gw = renew(0, g_w[i], head_size)
        uw = renew(1, u_w[i], head_size)
        dw = renew(2, d_w[i].T, hidden)

        def some(r, inner):
            span = pl.ds(pl.multiple_of(r * chunk, chunk), chunk)
            qn = unit(q[i, span].astype(F32)).astype(BF16)
            gate_pre = dot(qn, gw)
            hid = (gate_pre * jax.nn.sigmoid(gate_pre) * dot(qn, uw)).astype(BF16)
            fast = dot(hid, dw, ((1,), (1,)))
            comb[span, pl.ds(pl.multiple_of(i * head_size, head_size), head_size)] = (att[i, span] + fast).astype(BF16)
            return inner

        lax.fori_loop(0, rows // chunk, some, 0)
        return carry

    lax.fori_loop(0, heads, apply, 0)

    loads[7].wait()
    out_rows = out.shape[0]
    piece_cols = out.shape[1] // len(trees)

    def rs_copy(p, spot):
        axis, sign = trees[p][spot]
        k = p * 16 + slot(spot)
        return pltpu.make_async_remote_copy(
            src_ref=go_out.at[k], dst_ref=come_in.at[k], send_sem=rs_send.at[k], recv_sem=rs_recv.at[k],
            device_id=at((axis, -sign)), device_id_type=MESH,
        )

    def gathered(p, spot):
        own = part[p, pl.ds(pl.multiple_of(owner(spot) * out_rows, out_rows), out_rows)]
        for child in belows[p].get(spot, []):
            rs_copy(p, child).wait_recv()
            own = own + come_in[p * 16 + slot(child)].astype(F32)
        return own.astype(BF16)

    ready = set()
    for p, spot in order[::-1]:
        if p not in ready:
            ready.add(p)

            def cols(j, carry, p=p):
                lanes = pl.ds(pl.multiple_of(j * 256, 256), 256)
                wide = pl.ds(pl.multiple_of(p * piece_cols + j * 256, 256), 256)
                part[p, :, lanes] = dot(comb[...], w_o[:, wide])
                return carry

            lax.fori_loop(0, piece_cols // 256, cols, 0)
        go_out[p * 16 + slot(spot)] = gathered(p, spot)
        rs_copy(p, spot).start()
    for p in range(len(trees)):
        out[:, p * piece_cols:(p + 1) * piece_cols] = gathered(p, (0, 0))

    for p, spot in order:
        ag_copy(p, spot).wait_send()
        rs_copy(p, spot).wait_send()
    for c in halo + scatter + share:
        c.wait_send()


def shards(
    tok_n, head_n, tokens, w_query, w_key, w_value, w_out, fast_gate, fast_up, fast_down, token_rate, head_step
):
    rows, width = tokens.shape
    depth, local_width = w_query.shape
    d_model = w_out.shape[1]
    heads, head_size, hidden = fast_gate.shape
    pieces = len(MIRRORS)
    any_space = pl.BlockSpec(memory_space=pl.ANY)
    vmem = pl.BlockSpec(memory_space=pltpu.VMEM)
    smem = pl.BlockSpec(memory_space=pltpu.SMEM)
    dma = pltpu.SemaphoreType.DMA
    return pl.pallas_call(
        functools.partial(kernel, tok_n),
        out_shape=jax.ShapeDtypeStruct((rows // head_n, d_model), BF16),
        in_specs=[any_space] * 8 + [vmem, smem],
        out_specs=vmem,
        scratch_shapes=[
            pltpu.VMEM((head_n, rows, width), BF16),
            pltpu.VMEM((3, depth, local_width), BF16),
            pltpu.VMEM((local_width, d_model), BF16),
            pltpu.VMEM((3, rows, local_width), F32),
            pltpu.VMEM((heads, rows, head_size), BF16),
            pltpu.VMEM((2 * heads, WINDOW + rows, head_size), BF16),
            pltpu.VMEM((heads, head_size, hidden), F32),
            pltpu.VMEM((heads, head_size, hidden), F32),
            pltpu.VMEM((heads, hidden, head_size), F32),
            pltpu.VMEM((rows, head_size), BF16),
            pltpu.VMEM((rows, head_size), BF16),
            pltpu.VMEM((rows, hidden), BF16),
            pltpu.VMEM((rows, hidden), BF16),
            pltpu.VMEM((rows, hidden), BF16),
            pltpu.VMEM((heads * 3 * head_size, hidden), BF16),
            pltpu.VMEM((tok_n, heads * 3 * head_size // tok_n, hidden), BF16),
            pltpu.VMEM((heads * 3 * head_size, hidden), BF16),
            pltpu.VMEM((heads, rows, head_size), F32),
            pltpu.VMEM((rows, local_width), BF16),
            pltpu.VMEM((pieces, rows, d_model // pieces), F32),
            pltpu.VMEM((pieces * 16, rows // head_n, d_model // pieces), BF16),
            pltpu.VMEM((pieces * 16, rows // head_n, d_model // pieces), BF16),
            dma((8,)), dma((pieces * 16,)), dma((pieces * 16,)), dma((2 * heads,)), dma((2 * heads,)),
            dma((2 * tok_n,)), dma((2 * tok_n,)), dma((pieces * 16,)), dma((pieces * 16,)),
        ],
        compiler_params=pltpu.CompilerParams(
            collective_id=0, has_side_effects=True, vmem_limit_bytes=60 * 2**20
        ),
    )(tokens, w_query, w_key, w_value, w_out, fast_gate, fast_up, fast_down, token_rate, head_step)


def solution(mesh):
    placed = (
        P("tok", "head"),
        P(None, "head"),
        P(None, "head"),
        P(None, "head"),
        P("head", None),
        P("head", None, None),
        P("head", None, None),
        P("head", None, None),
        P("tok", "head"),
        P("head"),
    )
    return jax.shard_map(
        functools.partial(shards, mesh.shape["tok"], mesh.shape["head"]),
        mesh=mesh, in_specs=placed, out_specs=P(("tok", "head"), None), check_vma=False,
    )
```

time: 349 us -> 113 us (0.32)
  the two profiles are of different devices: /device:TPU:1 before, /device:TPU:58 now
where the time goes in v1:
time: 113 us
  Pallas kernels  110 us (97%)
  local copies, waits for them, and re-layouts  3.21 us (3%)
    pallas_call x1, Pallas kernels, shards(): pl.pallas_call(functools.partial(kernel, tok_n), out_shape=jax.ShapeDtype...  110 us
    unnamed x2, local copies, waits for them, and re-layouts  3.21 us

profile of v1, /device:TPU:58, one launch (start us, length us, event | category | flops | bytes accessed | tf_op | source)
XLA Modules:
  0.0 113.3 jit_solution(1459224619888526756)
XLA Ops:
  0.0 1.5 %copy.11.rate = f32[512,2]{1,0:T(8,128)} copy(f32[512,2]{0,1:T(2,128)} %param.18) | data formatting | bytes 8192 | tf_op args[8]
  1.5 110.1 %shard_map.100 = bf16[32,4096]{1,0:T(8,128)(2,1)} custom-call(bf16[512,256]{1,0:T(8,128)(2,1)} %tokens.1, bf16[4096,256]{1,0:T(8,128)(2,1)} %w_query.1, bf16[4096,256]{1,0:T(8,128)(2,1)} %w_key.1, bf16[4096,256]{1,0:T(8,128)(2,1)} %w_value.1, bf16[256,4096]{1,0:T(8,128)(2,1)} %w_out.1, f32[2,128,256]{2,1,0:T(8,128)} %gate.1, f32[2,128,256]{2,1,0:T(8,128)} %upper.1, ...), custom_call_target="tpu_custom_call" | custom-call | tf_op jit(solution)/shard_map/pallas_call | solution.py:358
  111.6 1.7 %copy.13 = bf16[32,4096]{1,0:T(8,128)(2,1)} copy(bf16[32,4096]{1,0:T(8,128)(2,1)} %shard_map.100) | data formatting | bytes 524288

commit v2 on v1

--- a/solution.py
+++ b/solution.py
@@ -85,8 +85,8 @@
 def kernel(
     tok_n, tokens, w_query, w_key, w_value, w_out, gate, upper, down, rate, step,
     out,
-    blocks, w_in, w_o, acc, q, kv, g_w, u_w, d_w, kn_s, tg_s, hid_s, dup_s, dgate_s,
-    grad, grad_in, grad_sum, att, comb, part, come_in, go_out,
+    blocks, w_in, w_o, acc, q, kv, g_w, u_w, d_w,
+    grad, pair_in, half, chip_in, grad_sum, att, comb, part, come_in, go_out,
     load_sem, ag_send, ag_recv, halo_send, halo_recv, ar_send, ar_recv, rs_send, rs_recv,
 ):
     rows = tokens.shape[0]
@@ -123,9 +123,10 @@
     ways = [("x", 1), ("x", -1), ("z", 1), ("z", -1)]
     for way in ways:
         pl.semaphore_signal(barrier, inc=1, device_id=at(way), device_id_type=MESH)
-    for k in range(1, tok_n):
+    near = [1, tok_n - 1] + list(range(2, tok_n, 2))
+    for k in near:
         pl.semaphore_signal(barrier, inc=1, device_id=tok_at(k), device_id_type=MESH)
-    pl.semaphore_wait(barrier, len(ways) + tok_n - 1)
+    pl.semaphore_wait(barrier, len(ways) + len(near))
 
     trees = [tree_of(*m) for m in MIRRORS]
     belows = [below_of(tr) for tr in trees]
@@ -181,65 +182,89 @@
             send_sem=halo_send.at[i], recv_sem=halo_recv.at[i], device_id=tok_at(1), device_id_type=MESH,
         ))
         halo[-1].start()
-    for i in range(heads):
-        q[i] = acc[0, :, i * head_size:(i + 1) * head_size].astype(BF16)
 
     for c in loads[4:7]:
         c.wait()
-    chunk = 128
-
-    def grads(i, carry):
+    core = lax.rem(t, 2)
+    chip = t // 2
+    chips = tok_n // 2
+    other = (t + 1 - 2 * core, h)
+    half_rows = head_size // 2
+    own_half = pl.ds(pl.multiple_of(core * half_rows, half_rows), half_rows)
+    other_half = pl.ds(pl.multiple_of((1 - core) * half_rows, half_rows), half_rows)
+    cut_rows, cut_cols = 2 * half_rows // chips, 3 * hidden // 2
+
+    def cut(s, base=0):
+        return (
+            pl.ds(pl.multiple_of(base + (s // 2) * cut_rows, cut_rows), cut_rows),
+            pl.ds(pl.multiple_of(lax.rem(s, 2) * cut_cols, cut_cols), cut_cols),
+        )
+
+    def column(row):
+        n = row.shape[1]
+        wide = jnp.broadcast_to(row, (n, n))
+        eye = lax.broadcasted_iota(jnp.int32, (n, n), 0) == lax.broadcasted_iota(jnp.int32, (n, n), 1)
+        return jnp.sum(jnp.where(eye, wide, 0.0), axis=1, keepdims=True)
+
+    def ar_copy(kind, i, src, dst, to):
+        k = kind * heads + i
+        return pltpu.make_async_remote_copy(
+            src_ref=src, dst_ref=dst, send_sem=ar_send.at[k], recv_sem=ar_recv.at[k], device_id=to, device_id_type=MESH,
+        )
+
+    pair = [ar_copy(0, i, grad.at[i, other_half], pair_in.at[i], other) for i in range(heads)]
+    here = pl.ds(WINDOW, rows)
+    for i in range(heads):
         gw = g_w[i].astype(BF16)
         uw = u_w[i].astype(BF16)
         dw = d_w[i].astype(BF16)
-
-        def some(r, inner):
-            span = pl.ds(pl.multiple_of(r * chunk, chunk), chunk)
-            here = pl.ds(pl.multiple_of(r * chunk, chunk) + WINDOW, chunk)
-            kn = unit(kv[i, here].astype(F32)).astype(BF16)
-            each = rate[span]
-            lane = lax.broadcasted_iota(jnp.int32, each.shape, 1)
-            mine = jnp.sum(jnp.where(lane == i, each, 0.0), axis=1, keepdims=True)
-            tg = (-mine * kv[heads + i, here].astype(F32)).astype(BF16)
-            gate_pre = dot(kn, gw)
-            up_pre = dot(kn, uw)
-            back = dot(tg, dw, ((1,), (1,)))
-            sigma = jax.nn.sigmoid(gate_pre)
-            active = gate_pre * sigma
-            kn_s[span] = kn
-            tg_s[span] = tg
-            hid_s[span] = (active * up_pre).astype(BF16)
-            dup_s[span] = (back * active).astype(BF16)
-            dgate_s[span] = (back * up_pre * sigma * (1.0 + gate_pre * (1.0 - sigma))).astype(BF16)
-            return inner
-
-        lax.fori_loop(0, rows // chunk, some, 0)
-        base = pl.multiple_of(i * (3 * head_size), head_size)
-        kn_all = kn_s[...]
-        grad[pl.ds(base, head_size)] = dot(kn_all, dgate_s[...], ((0,), (0,))).astype(BF16)
-        grad[pl.ds(base + head_size, head_size)] = dot(kn_all, dup_s[...], ((0,), (0,))).astype(BF16)
-        grad[pl.ds(base + 2 * head_size, head_size)] = dot(tg_s[...], hid_s[...], ((0,), (0,))).astype(BF16)
-        return carry
-
-    lax.fori_loop(0, heads, grads, 0)
-
-    slice_rows = grad.shape[0] // tok_n
-    scatter = []
-    for k in range(1, tok_n):
-        to = lax.rem(t + k, tok_n)
-        scatter.append(pltpu.make_async_remote_copy(
-            src_ref=grad.at[pl.ds(pl.multiple_of(to * slice_rows, slice_rows), slice_rows)], dst_ref=grad_in.at[k],
-            send_sem=ar_send.at[k], recv_sem=ar_recv.at[k], device_id=(to, h), device_id_type=MESH,
-        ))
-        scatter[-1].start()
+        kn = unit(kv[i, here].astype(F32)).astype(BF16)
+        each = jnp.concatenate([column(rate[i:i + 1, r:r + 128]) for r in range(0, rows, 128)], axis=0)
+        tg = (-each * kv[heads + i, here].astype(F32)).astype(BF16)
+        gate_pre = dot(kn, gw)
+        up_pre = dot(kn, uw)
+        back = dot(tg, dw, ((1,), (1,)))
+        sigma = jax.nn.sigmoid(gate_pre)
+        active = gate_pre * sigma
+        hid = (active * up_pre).astype(BF16)
+        d_up = (back * active).astype(BF16)
+        d_gate = (back * up_pre * sigma * (1.0 + gate_pre * (1.0 - sigma))).astype(BF16)
+        grad[i, :, 0:hidden] = dot(kn, d_gate, ((0,), (0,))).astype(BF16)
+        grad[i, :, hidden:2 * hidden] = dot(kn, d_up, ((0,), (0,))).astype(BF16)
+        grad[i, :, 2 * hidden:] = dot(tg, hid, ((0,), (0,))).astype(BF16)
+        pair[i].start()
+    for i in range(heads):
+        q[i] = acc[0, :, i * head_size:(i + 1) * head_size].astype(BF16)
+
+    cross = []
+    for i in range(heads):
+        pair[i].wait_recv()
+        half[i] = (grad[i, own_half].astype(F32) + pair_in[i].astype(F32)).astype(BF16)
+        for k in range(1, chips):
+            to = lax.rem(chip + k, chips)
+            cross.append(ar_copy(1 + k, i, half.at[(i,) + cut(to)], chip_in.at[i, k], (to * 2 + core, h)))
+            cross[-1].start()
+    back_to = []
+    mine = cut(chip, core * half_rows)
+    for i in range(heads):
+        total = half[(i,) + cut(chip)].astype(F32)
+        for k in range(1, chips):
+            cross[i * (chips - 1) + k - 1].wait_recv()
+            total = total + chip_in[i, k].astype(F32)
+        grad_sum[(i,) + mine] = total.astype(BF16)
+        for k in range(1, chips):
+            to = lax.rem(chip + k, chips)
+            spot = grad_sum.at[(i,) + mine]
+            back_to.append(ar_copy(chips + k, i, spot, spot, (to * 2 + core, h)))
+            back_to[-1].start()
 
     def attend(i):
+        chunk = 128
         keys_n = WINDOW + chunk
-
-        def some(b, carry):
-            first = pl.multiple_of(b * chunk, chunk)
-            keys = kv[i, pl.ds(first, keys_n)]
-            scores = dot(q[i, pl.ds(first, chunk)], keys, ((1,), (1,))) * head_size ** (-0.5)
+        for b in range(rows // chunk):
+            first = b * chunk
+            keys = kv[i, first:first + keys_n]
+            scores = dot(q[i, first:first + chunk], keys, ((1,), (1,))) * head_size ** (-0.5)
             r = lax.broadcasted_iota(jnp.int32, scores.shape, 0)
             c = lax.broadcasted_iota(jnp.int32, scores.shape, 1)
             allowed = (c > r) & (c <= r + WINDOW) & (c >= WINDOW - first - t * rows)
@@ -247,58 +272,36 @@
             top = jnp.max(scores, axis=-1, keepdims=True)
             expo = jnp.exp(scores - top)
             weights = (expo * (1.0 / jnp.sum(expo, axis=-1, keepdims=True))).astype(BF16)
-            att[i, pl.ds(first, chunk)] = dot(weights, kv[heads + i, pl.ds(first, keys_n)])
-            return carry
-
-        lax.fori_loop(0, rows // chunk, some, 0)
+            att[i, first:first + chunk] = dot(weights, kv[heads + i, first:first + keys_n])
 
     for c in halo:
         c.wait_recv()
-    attend(0)
-
-    mine = pl.ds(pl.multiple_of(t * slice_rows, slice_rows), slice_rows)
-    total = grad[mine].astype(F32)
-    for k, c in enumerate(scatter, 1):
-        c.wait_recv()
-        total = total + grad_in[k].astype(F32)
-    grad_sum[mine] = total.astype(BF16)
-    share = []
-    for k in range(1, tok_n):
-        share.append(pltpu.make_async_remote_copy(
-            src_ref=grad_sum.at[mine], dst_ref=grad_sum.at[mine],
-            send_sem=ar_send.at[tok_n + k], recv_sem=ar_recv.at[tok_n + k], device_id=tok_at(k), device_id_type=MESH,
-        ))
-        share[-1].start()
-    for i in range(1, heads):
+    for i in range(heads):
         attend(i)
-    for c in share:
-        c.wait_recv()
-
-    def apply(i, carry):
-        base = pl.multiple_of(i * (3 * head_size), head_size)
+    last = []
+    for i in range(heads):
+        for k in range(1, chips):
+            back_to[i * (chips - 1) + k - 1].wait_recv()
+        spot = grad_sum.at[i, own_half]
+        last.append(ar_copy(2 * chips, i, spot, spot, other))
+        last[-1].start()
+
+    for i in range(heads):
+        last[i].wait_recv()
 
         def renew(j, matrix, fan_in):
-            g = grad_sum[pl.ds(base + j * head_size, head_size)].astype(F32)
+            g = grad_sum[i, :, j * hidden:(j + 1) * hidden].astype(F32)
             mean_sq = jnp.sum(jnp.sum(g * g, axis=1, keepdims=True), axis=0, keepdims=True) / (head_size * hidden)
             return (matrix - (step[i] * fan_in ** (-0.5)) * g * lax.rsqrt(mean_sq + 1e-06)).astype(BF16)
 
         gw = renew(0, g_w[i], head_size)
         uw = renew(1, u_w[i], head_size)
         dw = renew(2, d_w[i].T, hidden)
-
-        def some(r, inner):
-            span = pl.ds(pl.multiple_of(r * chunk, chunk), chunk)
-            qn = unit(q[i, span].astype(F32)).astype(BF16)
-            gate_pre = dot(qn, gw)
-            hid = (gate_pre * jax.nn.sigmoid(gate_pre) * dot(qn, uw)).astype(BF16)
-            fast = dot(hid, dw, ((1,), (1,)))
-            comb[span, pl.ds(pl.multiple_of(i * head_size, head_size), head_size)] = (att[i, span] + fast).astype(BF16)
-            return inner
-
-        lax.fori_loop(0, rows // chunk, some, 0)
-        return carry
-
-    lax.fori_loop(0, heads, apply, 0)
+        qn = unit(q[i].astype(F32)).astype(BF16)
+        gate_pre = dot(qn, gw)
+        hid = (gate_pre * jax.nn.sigmoid(gate_pre) * dot(qn, uw)).astype(BF16)
+        fast = dot(hid, dw, ((1,), (1,)))
+        comb[:, i * head_size:(i + 1) * head_size] = (att[i] + fast).astype(BF16)
 
     loads[7].wait()
     out_rows = out.shape[0]
@@ -339,7 +342,7 @@
     for p, spot in order:
         ag_copy(p, spot).wait_send()
         rs_copy(p, spot).wait_send()
-    for c in halo + scatter + share:
+    for c in halo + pair + cross + back_to + last:
         c.wait_send()
 
 
@@ -370,26 +373,23 @@
             pltpu.VMEM((heads, head_size, hidden), F32),
             pltpu.VMEM((heads, head_size, hidden), F32),
             pltpu.VMEM((heads, hidden, head_size), F32),
-            pltpu.VMEM((rows, head_size), BF16),
-            pltpu.VMEM((rows, head_size), BF16),
-            pltpu.VMEM((rows, hidden), BF16),
-            pltpu.VMEM((rows, hidden), BF16),
-            pltpu.VMEM((rows, hidden), BF16),
-            pltpu.VMEM((heads * 3 * head_size, hidden), BF16),
-            pltpu.VMEM((tok_n, heads * 3 * head_size // tok_n, hidden), BF16),
-            pltpu.VMEM((heads * 3 * head_size, hidden), BF16),
+            pltpu.VMEM((heads, head_size, 3 * hidden), BF16),
+            pltpu.VMEM((heads, head_size // 2, 3 * hidden), BF16),
+            pltpu.VMEM((heads, head_size // 2, 3 * hidden), BF16),
+            pltpu.VMEM((heads, tok_n // 2, 2 * head_size // tok_n, 3 * hidden // 2), BF16),
+            pltpu.VMEM((heads, head_size, 3 * hidden), BF16),
             pltpu.VMEM((heads, rows, head_size), F32),
             pltpu.VMEM((rows, local_width), BF16),
             pltpu.VMEM((pieces, rows, d_model // pieces), F32),
             pltpu.VMEM((pieces * 16, rows // head_n, d_model // pieces), BF16),
             pltpu.VMEM((pieces * 16, rows // head_n, d_model // pieces), BF16),
             dma((8,)), dma((pieces * 16,)), dma((pieces * 16,)), dma((2 * heads,)), dma((2 * heads,)),
-            dma((2 * tok_n,)), dma((2 * tok_n,)), dma((pieces * 16,)), dma((pieces * 16,)),
+            dma(((tok_n + 1) * heads,)), dma(((tok_n + 1) * heads,)), dma((pieces * 16,)), dma((pieces * 16,)),
         ],
         compiler_params=pltpu.CompilerParams(
             collective_id=0, has_side_effects=True, vmem_limit_bytes=60 * 2**20
         ),
-    )(tokens, w_query, w_key, w_value, w_out, fast_gate, fast_up, fast_down, token_rate, head_step)
+    )(tokens, w_query, w_key, w_value, w_out, fast_gate, fast_up, fast_down, token_rate.T, head_step)
 
 
 def solution(mesh):

time: 113 us -> 107 us (0.947)
  the two profiles are of different devices: /device:TPU:58 before, /device:TPU:48 now
where the time goes in v2:
time: 107 us
  Pallas kernels  106 us (99%)
  local copies, waits for them, and re-layouts  1.67 us (2%)
    pallas_call x1, Pallas kernels, shards(): pl.pallas_call(functools.partial(kernel, tok_n), out_shape=jax.ShapeDtype...  106 us

profile of v2, /device:TPU:48, one launch (start us, length us, event | category | flops | bytes accessed | tf_op | source)
XLA Modules:
  0.0 107.2 jit_solution(3885770539695407914)
XLA Ops:
  0.0 105.6 %shard_map.100 = bf16[32,4096]{1,0:T(8,128)(2,1)} custom-call(bf16[512,256]{1,0:T(8,128)(2,1)} %tokens.1, bf16[4096,256]{1,0:T(8,128)(2,1)} %w_query.1, bf16[4096,256]{1,0:T(8,128)(2,1)} %w_key.1, bf16[4096,256]{1,0:T(8,128)(2,1)} %w_value.1, bf16[256,4096]{1,0:T(8,128)(2,1)} %w_out.1, f32[2,128,256]{2,1,0:T(8,128)} %gate.1, f32[2,128,256]{2,1,0:T(8,128)} %upper.1, ...), custom_call_target="tpu_custom_call" | custom-call | tf_op jit(solution)/shard_map/pallas_call | solution.py:361
  105.6 1.7 %copy.12 = bf16[32,4096]{1,0:T(8,128)(2,1)} copy(bf16[32,4096]{1,0:T(8,128)(2,1)} %shard_map.100) | data formatting | bytes 524288

commit v3 on v2

--- a/solution.py
+++ b/solution.py
@@ -11,6 +11,10 @@
 MESH = pl.DeviceIdType.MESH
 WINDOW = 512
 SIDE = 4
+RX, RZ, LX, LZ = 43.5e3, 21.7e3, 1.8, 3.5
+AHEAD = 2.0
+PART = 0.7
+LAG = 24
 F32 = jnp.float32
 BF16 = jnp.bfloat16
 MIRRORS = ((1, 1), (-1, 1), (1, -1), (-1, -1))
@@ -46,27 +50,71 @@
 
 
 def plan(trees, size):
-    rate = {"x": 46.8e3, "z": 23.4e3}
-    late = {"x": 1.8, "z": 2.6}
+    rate = {"x": RX, "z": RZ}
+    late = {"x": LX, "z": LZ}
     belows = [below_of(t) for t in trees]
-    free = {(a, s): 0.0 for a in "xz" for s in (1, -1)}
-    heap, count, order = [], 0, []
-
-    def send(when, piece, spot):
+    queue = {(a, s): [] for a in "xz" for s in (1, -1)}
+    free = dict.fromkeys(queue, 0.0)
+    heap, count, done = [], 0, []
+
+    def add(piece, spot):
         nonlocal count
-        for to in sorted(belows[piece].get(spot, []), key=lambda s: -height(belows[piece], s)):
-            way = trees[piece][to]
-            begin = max(when, free[way])
-            free[way] = begin + size / rate[way[0]]
+        for to in belows[piece].get(spot, []):
             count += 1
-            heapq.heappush(heap, (free[way] + late[way[0]], count, piece, to))
+            rank = -height(belows[piece], to)
+            heapq.heappush(queue[trees[piece][to]], (rank, count, piece, to))
+
+    def run(now):
+        nonlocal count
+        for way, waiting in queue.items():
+            if waiting and free[way] <= now:
+                _, _, piece, to = heapq.heappop(waiting)
+                free[way] = now + size / rate[way[0]]
+                count += 1
+                heapq.heappush(heap, (free[way], count, None))
+                count += 1
+                heapq.heappush(heap, (free[way] + late[way[0]], count, (now, piece, to)))
 
     for piece in range(len(trees)):
-        send(0.0, piece, (0, 0))
+        add(piece, (0, 0))
+    run(0.0)
     while heap:
-        when, _, piece, spot = heapq.heappop(heap)
-        order.append((piece, spot))
-        send(when, piece, spot)
+        now, _, got = heapq.heappop(heap)
+        if got:
+            done.append((got[0], now, got[1], got[2]))
+            add(got[1], got[2])
+        run(now)
+    return done
+
+
+def plan_back(trees, size, times):
+    rate = {"x": RX, "z": RZ}
+    late = {"x": LX, "z": LZ}
+    belows = [below_of(t) for t in trees]
+    rank = {(p, spot): -end for _, end, p, spot in times}
+    left = {(p, spot): len(belows[p].get(spot, [])) + 1 for p, spot in rank}
+    queue = {(a, s): [] for a in "xz" for s in (1, -1)}
+    free = dict.fromkeys(queue, 0.0)
+    heap = [(PART * (p + 1), p, (p, spot)) for p, spot in rank]
+    heapq.heapify(heap)
+    count, order = len(trees), []
+    while heap:
+        now, _, got = heapq.heappop(heap)
+        if got and got[1] != (0, 0):
+            left[got] -= 1
+            if left[got] == 0:
+                heapq.heappush(queue[trees[got[0]][got[1]]], (rank[got], got))
+        if heap and heap[0][0] == now:
+            continue
+        for way, waiting in queue.items():
+            if waiting and free[way] <= now:
+                _, (p, spot) = heapq.heappop(waiting)
+                free[way] = now + size / rate[way[0]]
+                order.append((now, p, spot))
+                count += 1
+                heapq.heappush(heap, (free[way], count, None))
+                count += 1
+                heapq.heappush(heap, (free[way] + late[way[0]], count, (p, from_of(spot, trees[p][spot]))))
     return order
 
 
@@ -96,11 +144,16 @@
     h = lax.axis_index("head")
     x, z = h // SIDE, lax.rem(h, SIDE)
 
-    def at(way):
+    def at_(way):
         axis, sign = way
         if axis == "x":
             return (t, lax.rem(x + (SIDE + sign), SIDE) * SIDE + z)
         return (t, x * SIDE + lax.rem(z + (SIDE + sign), SIDE))
+
+    nbr = {(a, s): at_((a, s)) for a in "xz" for s in (1, -1)}
+
+    def at(way):
+        return nbr[way]
 
     def owner(spot):
         a, b = spot
@@ -131,7 +184,14 @@
     trees = [tree_of(*m) for m in MIRRORS]
     belows = [below_of(tr) for tr in trees]
     piece_rows = rows // len(trees)
-    order = plan(trees, piece_rows * width * 2)
+    times = plan(trees, piece_rows * width * 2)
+    order = [(p, spot) for _, _, p, spot in times]
+    script = [(end, 0, p, spot) for _, end, p, spot in times]
+    came = {(p, spot): end for _, end, p, spot in times}
+    for begin, _, p, spot in times:
+        frm = from_of(spot, trees[p][spot])
+        script.append((max(begin - AHEAD, came.get((p, frm), -1.0)), 1, p, spot))
+    script.sort(key=lambda e: e[:2])
 
     def ag_copy(p, to):
         frm = from_of(to, trees[p][to])
@@ -143,12 +203,10 @@
             device_id=at(trees[p][to]), device_id_type=MESH,
         )
 
-    def ag_forward(p, spot):
-        for to in sorted(belows[p].get(spot, []), key=lambda s: -height(belows[p], s)):
-            ag_copy(p, to).start()
-
-    for p in range(len(trees)):
-        ag_forward(p, (0, 0))
+    early = [e for e in script if e[1] == 1 and e[0] <= 0.0]
+    script = [e for e in script if not (e[1] == 1 and e[0] <= 0.0)]
+    for _, _, p, spot in early:
+        ag_copy(p, spot).start()
 
     def project(spot, first):
         base = pl.multiple_of(owner(spot) * width, width)
@@ -164,9 +222,11 @@
         c.wait()
     project((0, 0), True)
     missing = {}
-    for p, spot in order:
+    for _, sends, p, spot in script:
+        if sends:
+            ag_copy(p, spot).start()
+            continue
         ag_copy(p, spot).wait_recv()
-        ag_forward(p, spot)
         missing[spot] = missing.get(spot, len(trees)) - 1
         if missing[spot] == 0:
             project(spot, False)
@@ -274,8 +334,12 @@
             weights = (expo * (1.0 / jnp.sum(expo, axis=-1, keepdims=True))).astype(BF16)
             att[i, first:first + chunk] = dot(weights, kv[heads + i, first:first + keys_n])
 
+    for p, spot in order:
+        ag_copy(p, spot).wait_send()
+    for c in pair + cross:
+        c.wait_send()
     for c in halo:
-        c.wait_recv()
+        c.wait()
     for i in range(heads):
         attend(i)
     last = []
@@ -286,8 +350,10 @@
         last.append(ar_copy(2 * chips, i, spot, spot, other))
         last[-1].start()
 
-    for i in range(heads):
-        last[i].wait_recv()
+    for c in back_to:
+        c.wait_send()
+    for i in range(heads):
+        last[i].wait()
 
         def renew(j, matrix, fan_in):
             g = grad_sum[i, :, j * hidden:(j + 1) * hidden].astype(F32)
@@ -322,27 +388,29 @@
             own = own + come_in[p * 16 + slot(child)].astype(F32)
         return own.astype(BF16)
 
-    ready = set()
-    for p, spot in order[::-1]:
-        if p not in ready:
-            ready.add(p)
-
-            def cols(j, carry, p=p):
-                lanes = pl.ds(pl.multiple_of(j * 256, 256), 256)
-                wide = pl.ds(pl.multiple_of(p * piece_cols + j * 256, 256), 256)
-                part[p, :, lanes] = dot(comb[...], w_o[:, wide])
-                return carry
-
-            lax.fori_loop(0, piece_cols // 256, cols, 0)
+    def fill(p):
+        def cols(j, carry):
+            lanes = pl.ds(pl.multiple_of(j * 256, 256), 256)
+            wide = pl.ds(pl.multiple_of(p * piece_cols + j * 256, 256), 256)
+            part[p, :, lanes] = dot(comb[...], w_o[:, wide])
+            return carry
+
+        lax.fori_loop(0, piece_cols // 256, cols, 0)
+
+    filled, sent = 0, []
+    for now, p, spot in plan_back(trees, out_rows * piece_cols * 2, times):
+        while filled < len(trees) and (filled <= p or now >= PART * (filled + 1)):
+            fill(filled)
+            filled += 1
         go_out[p * 16 + slot(spot)] = gathered(p, spot)
-        rs_copy(p, spot).start()
+        sent.append(rs_copy(p, spot))
+        sent[-1].start()
+        if len(sent) > LAG:
+            sent[-1 - LAG].wait_send()
     for p in range(len(trees)):
         out[:, p * piece_cols:(p + 1) * piece_cols] = gathered(p, (0, 0))
 
-    for p, spot in order:
-        ag_copy(p, spot).wait_send()
-        rs_copy(p, spot).wait_send()
-    for c in halo + pair + cross + back_to + last:
+    for c in sent[-LAG:]:
         c.wait_send()
 
 

time: 107 us -> 96.5 us (0.902)
  the two profiles are of different devices: /device:TPU:48 before, /device:TPU:1 now
where the time goes in v3:
time: 96.5 us; the launch traced here: 96.4 us
  Pallas kernels  94.7 us (98%)
  local copies, waits for them, and re-layouts  1.67 us (2%)
    pallas_call x1, Pallas kernels, shards(): pl.pallas_call(functools.partial(kernel, tok_n), out_shape=jax.ShapeDtype...  94.7 us

profile of v3, /device:TPU:1, one launch (start us, length us, event | category | flops | bytes accessed | tf_op | source)
XLA Modules:
  0.0 96.4 jit_solution(8855970734487657881)
XLA Ops:
  0.0 94.7 %shard_map.100 = bf16[32,4096]{1,0:T(8,128)(2,1)} custom-call(bf16[512,256]{1,0:T(8,128)(2,1)} %tokens.1, bf16[4096,256]{1,0:T(8,128)(2,1)} %w_query.1, bf16[4096,256]{1,0:T(8,128)(2,1)} %w_key.1, bf16[4096,256]{1,0:T(8,128)(2,1)} %w_value.1, bf16[256,4096]{1,0:T(8,128)(2,1)} %w_out.1, f32[2,128,256]{2,1,0:T(8,128)} %gate.1, f32[2,128,256]{2,1,0:T(8,128)} %upper.1, ...), custom_call_target="tpu_custom_call" | custom-call | tf_op jit(solution)/shard_map/pallas_call | solution.py:429
  94.7 1.7 %copy.12 = bf16[32,4096]{1,0:T(8,128)(2,1)} copy(bf16[32,4096]{1,0:T(8,128)(2,1)} %shard_map.100) | data formatting | bytes 524288

commit v4 on v3

--- a/solution.py
+++ b/solution.py
@@ -13,8 +13,10 @@
 SIDE = 4
 RX, RZ, LX, LZ = 43.5e3, 21.7e3, 1.8, 3.5
 AHEAD = 2.0
-PART = 0.7
-LAG = 24
+PART = 1.2
+LATE = 4.0
+UNIT = 0.25
+AG_SEMS, RS_SEMS = 51, 32
 F32 = jnp.float32
 BF16 = jnp.bfloat16
 MIRRORS = ((1, 1), (-1, 1), (1, -1), (-1, -1))
@@ -135,7 +137,7 @@
     out,
     blocks, w_in, w_o, acc, q, kv, g_w, u_w, d_w,
     grad, pair_in, half, chip_in, grad_sum, att, comb, part, come_in, go_out,
-    load_sem, ag_send, ag_recv, halo_send, halo_recv, ar_send, ar_recv, rs_send, rs_recv,
+    load_sem, ag_send, ag_recv, halo_sem, ar_send, ar_recv, rs_send, rs_recv,
 ):
     rows = tokens.shape[0]
     width = tokens.shape[1]
@@ -162,13 +164,16 @@
     def tok_at(k):
         return (lax.rem(t + k, tok_n), h)
 
+    def drain(ref, sem):
+        pltpu.make_async_copy(ref, ref, sem).wait()
+
     loads = [pltpu.make_async_copy(tokens, blocks.at[0], load_sem.at[0])]
     for j, w in enumerate((w_query, w_key, w_value)):
-        loads.append(pltpu.make_async_copy(w, w_in.at[j], load_sem.at[1 + j]))
-    loads.append(pltpu.make_async_copy(gate, g_w, load_sem.at[4]))
-    loads.append(pltpu.make_async_copy(upper, u_w, load_sem.at[5]))
-    loads.append(pltpu.make_async_copy(down, d_w, load_sem.at[6]))
-    loads.append(pltpu.make_async_copy(w_out, w_o, load_sem.at[7]))
+        loads.append(pltpu.make_async_copy(w, w_in.at[j], load_sem.at[1]))
+    loads.append(pltpu.make_async_copy(gate, g_w, load_sem.at[2]))
+    loads.append(pltpu.make_async_copy(upper, u_w, load_sem.at[3]))
+    loads.append(pltpu.make_async_copy(down, d_w, load_sem.at[4]))
+    loads.append(pltpu.make_async_copy(w_out, w_o, load_sem.at[5]))
     for c in loads:
         c.start()
 
@@ -193,13 +198,24 @@
         script.append((max(begin - AHEAD, came.get((p, frm), -1.0)), 1, p, spot))
     script.sort(key=lambda e: e[:2])
 
+    finish = {}
+    for p, spot in order:
+        finish[spot] = max(finish.get(spot, 0.0), came[p, spot])
+    late = [spot for spot in finish if finish[spot] > max(finish.values()) - LATE]
+    shared, seat = {}, {}
+    for p, spot in order:
+        if spot not in late and spot not in belows[p]:
+            shared.setdefault(spot, []).append(p)
+    for p, spot in order:
+        key = spot if p in shared.get(spot, []) else (p, spot)
+        seat[p, spot] = seat.setdefault(key, len(set(seat.values())))
+
     def ag_copy(p, to):
         frm = from_of(to, trees[p][to])
         span = pl.ds(p * piece_rows, piece_rows)
         src = tokens.at[span] if frm == (0, 0) else blocks.at[slot(frm), span]
-        k = p * 16 + slot(to)
         return pltpu.make_async_remote_copy(
-            src_ref=src, dst_ref=blocks.at[slot(to), span], send_sem=ag_send.at[k], recv_sem=ag_recv.at[k],
+            src_ref=src, dst_ref=blocks.at[slot(to), span], send_sem=ag_send.at[0], recv_sem=ag_recv.at[seat[p, to]],
             device_id=at(trees[p][to]), device_id_type=MESH,
         )
 
@@ -208,40 +224,64 @@
     for _, _, p, spot in early:
         ag_copy(p, spot).start()
 
-    def project(spot, first):
+    def project(spot, span, low, high, first=False):
         base = pl.multiple_of(owner(spot) * width, width)
 
         def one(j, carry):
-            prod = dot(blocks[slot(spot)], w_in[j, pl.ds(base, width)])
-            acc[j] = prod if first else acc[j] + prod
+            prod = dot(blocks[slot(spot), span], w_in[j, pl.ds(base, width)])
+            acc[j, span] = prod if first else acc[j, span] + prod
             return carry
 
-        lax.fori_loop(0, 3, one, 0)
-
-    for c in loads[:4]:
-        c.wait()
-    project((0, 0), True)
-    missing = {}
-    for _, sends, p, spot in script:
+        if high == low + 1:
+            one(low, 0)
+        else:
+            lax.fori_loop(low, high, one, 0)
+
+    every = slice(0, rows)
+    loads[0].wait()
+    drain(w_in, load_sem.at[1])
+    project((0, 0), every, 0, 3, True)
+    missing = dict.fromkeys(finish, len(trees))
+    work, later, clock = [], [], 0.0
+    for n, (now, sends, p, spot) in enumerate(script):
+        clock = max(clock, now)
         if sends:
             ag_copy(p, spot).start()
-            continue
-        ag_copy(p, spot).wait_recv()
-        missing[spot] = missing.get(spot, len(trees)) - 1
-        if missing[spot] == 0:
-            project(spot, False)
+        else:
+            missing[spot] -= 1
+            group = shared.get(spot, [])
+            if p not in group:
+                ag_copy(p, spot).wait_recv()
+            elif came[p, spot] == max(came[g, spot] for g in group) and p == max(
+                g for g in group if came[g, spot] == came[p, spot]
+            ):
+                drain(blocks.at[slot(spot), pl.ds(0, len(group) * piece_rows)], ag_recv.at[seat[p, spot]])
+            if spot in late:
+                work.append((spot, slice(p * piece_rows, (p + 1) * piece_rows), 1))
+                work.append((spot, slice(p * piece_rows, (p + 1) * piece_rows), 2))
+                if missing[spot] == 0:
+                    later.append((spot, every, 0))
+            elif missing[spot] == 0:
+                work.append((spot, every, 1))
+                work.append((spot, every, 2))
+                later.append((spot, every, 0))
+        until = script[n + 1][0] if n + 1 < len(script) else clock
+        while (work or later) and clock + UNIT / 2 <= until:
+            where, span, j = (work or later).pop(0)
+            project(where, span, j, j + 1)
+            clock += UNIT if span is every else UNIT / 2
+    for where, span, j in work:
+        project(where, span, j, j + 1)
 
     for i in range(heads):
         cols = slice(i * head_size, (i + 1) * head_size)
         kv[i, pl.ds(WINDOW, rows)] = acc[1, :, cols].astype(BF16)
         kv[heads + i, pl.ds(WINDOW, rows)] = acc[2, :, cols].astype(BF16)
-    halo = []
     for i in range(2 * heads):
-        halo.append(pltpu.make_async_remote_copy(
+        pltpu.make_async_remote_copy(
             src_ref=kv.at[i, pl.ds(rows, WINDOW)], dst_ref=kv.at[i, pl.ds(0, WINDOW)],
-            send_sem=halo_send.at[i], recv_sem=halo_recv.at[i], device_id=tok_at(1), device_id_type=MESH,
-        ))
-        halo[-1].start()
+            send_sem=halo_sem.at[0], recv_sem=halo_sem.at[1], device_id=tok_at(1), device_id_type=MESH,
+        ).start()
 
     for c in loads[4:7]:
         c.wait()
@@ -267,9 +307,9 @@
         return jnp.sum(jnp.where(eye, wide, 0.0), axis=1, keepdims=True)
 
     def ar_copy(kind, i, src, dst, to):
-        k = kind * heads + i
         return pltpu.make_async_remote_copy(
-            src_ref=src, dst_ref=dst, send_sem=ar_send.at[k], recv_sem=ar_recv.at[k], device_id=to, device_id_type=MESH,
+            src_ref=src, dst_ref=dst, send_sem=ar_send.at[kind], recv_sem=ar_recv.at[kind * heads + i],
+            device_id=to, device_id_type=MESH,
         )
 
     pair = [ar_copy(0, i, grad.at[i, other_half], pair_in.at[i], other) for i in range(heads)]
@@ -293,30 +333,28 @@
         grad[i, :, hidden:2 * hidden] = dot(kn, d_up, ((0,), (0,))).astype(BF16)
         grad[i, :, 2 * hidden:] = dot(tg, hid, ((0,), (0,))).astype(BF16)
         pair[i].start()
+    for where, span, j in later:
+        project(where, span, j, j + 1)
     for i in range(heads):
         q[i] = acc[0, :, i * head_size:(i + 1) * head_size].astype(BF16)
 
-    cross = []
     for i in range(heads):
         pair[i].wait_recv()
         half[i] = (grad[i, own_half].astype(F32) + pair_in[i].astype(F32)).astype(BF16)
         for k in range(1, chips):
             to = lax.rem(chip + k, chips)
-            cross.append(ar_copy(1 + k, i, half.at[(i,) + cut(to)], chip_in.at[i, k], (to * 2 + core, h)))
-            cross[-1].start()
-    back_to = []
+            ar_copy(1, i, half.at[(i,) + cut(to)], chip_in.at[i, k], (to * 2 + core, h)).start()
     mine = cut(chip, core * half_rows)
     for i in range(heads):
         total = half[(i,) + cut(chip)].astype(F32)
+        drain(chip_in.at[i, pl.ds(1, chips - 1)], ar_recv.at[heads + i])
         for k in range(1, chips):
-            cross[i * (chips - 1) + k - 1].wait_recv()
             total = total + chip_in[i, k].astype(F32)
         grad_sum[(i,) + mine] = total.astype(BF16)
         for k in range(1, chips):
             to = lax.rem(chip + k, chips)
             spot = grad_sum.at[(i,) + mine]
-            back_to.append(ar_copy(chips + k, i, spot, spot, (to * 2 + core, h)))
-            back_to[-1].start()
+            ar_copy(2, i, spot, spot, (to * 2 + core, h)).start()
 
     def attend(i):
         chunk = 128
@@ -334,26 +372,18 @@
             weights = (expo * (1.0 / jnp.sum(expo, axis=-1, keepdims=True))).astype(BF16)
             att[i, first:first + chunk] = dot(weights, kv[heads + i, first:first + keys_n])
 
-    for p, spot in order:
-        ag_copy(p, spot).wait_send()
-    for c in pair + cross:
-        c.wait_send()
-    for c in halo:
-        c.wait()
+    drain(kv.at[:, pl.ds(0, WINDOW)], halo_sem.at[1])
     for i in range(heads):
         attend(i)
     last = []
     for i in range(heads):
-        for k in range(1, chips):
-            back_to[i * (chips - 1) + k - 1].wait_recv()
+        drain(chip_in.at[i, pl.ds(1, chips - 1)], ar_recv.at[2 * heads + i])
         spot = grad_sum.at[i, own_half]
-        last.append(ar_copy(2 * chips, i, spot, spot, other))
+        last.append(ar_copy(3, i, spot, spot, other))
         last[-1].start()
 
-    for c in back_to:
-        c.wait_send()
-    for i in range(heads):
-        last[i].wait()
+    for i in range(heads):
+        last[i].wait_recv()
 
         def renew(j, matrix, fan_in):
             g = grad_sum[i, :, j * hidden:(j + 1) * hidden].astype(F32)
@@ -373,19 +403,33 @@
     out_rows = out.shape[0]
     piece_cols = out.shape[1] // len(trees)
 
+    node = {}
+    for p in range(len(trees)):
+        for spot in belows[p]:
+            node[p, spot] = len(node)
+
     def rs_copy(p, spot):
         axis, sign = trees[p][spot]
-        k = p * 16 + slot(spot)
+        frm = from_of(spot, trees[p][spot])
+        k = seats[p, frm] + belows[p][frm].index(spot)
         return pltpu.make_async_remote_copy(
-            src_ref=go_out.at[k], dst_ref=come_in.at[k], send_sem=rs_send.at[k], recv_sem=rs_recv.at[k],
+            src_ref=go_out.at[p * 16 + slot(spot)], dst_ref=come_in.at[k],
+            send_sem=rs_send.at[0], recv_sem=rs_recv.at[node[p, frm]],
             device_id=at((axis, -sign)), device_id_type=MESH,
         )
 
+    seats, taken = {}, 0
+    for p, spot in node:
+        seats[p, spot] = taken
+        taken += len(belows[p][spot])
+
     def gathered(p, spot):
         own = part[p, pl.ds(pl.multiple_of(owner(spot) * out_rows, out_rows), out_rows)]
-        for child in belows[p].get(spot, []):
-            rs_copy(p, child).wait_recv()
-            own = own + come_in[p * 16 + slot(child)].astype(F32)
+        n = len(belows[p].get(spot, []))
+        if n:
+            drain(come_in.at[pl.ds(seats[p, spot], n)], rs_recv.at[node[p, spot]])
+            for k in range(n):
+                own = own + come_in[seats[p, spot] + k].astype(F32)
         return own.astype(BF16)
 
     def fill(p):
@@ -397,21 +441,21 @@
 
         lax.fori_loop(0, piece_cols // 256, cols, 0)
 
-    filled, sent = 0, []
+    filled = 0
     for now, p, spot in plan_back(trees, out_rows * piece_cols * 2, times):
         while filled < len(trees) and (filled <= p or now >= PART * (filled + 1)):
             fill(filled)
             filled += 1
         go_out[p * 16 + slot(spot)] = gathered(p, spot)
-        sent.append(rs_copy(p, spot))
-        sent[-1].start()
-        if len(sent) > LAG:
-            sent[-1 - LAG].wait_send()
+        rs_copy(p, spot).start()
     for p in range(len(trees)):
         out[:, p * piece_cols:(p + 1) * piece_cols] = gathered(p, (0, 0))
 
-    for c in sent[-LAG:]:
-        c.wait_send()
+    drain(blocks.at[pl.ds(0, blocks.shape[0] - 1)], ag_send.at[0])
+    drain(kv.at[:, pl.ds(0, WINDOW)], halo_sem.at[0])
+    for kind, ref in enumerate((pair_in, chip_in.at[:, pl.ds(1, chips - 1)], chip_in.at[:, pl.ds(1, chips - 1)], pair_in)):
+        drain(ref, ar_send.at[kind])
+    drain(come_in.at[pl.ds(0, taken)], rs_send.at[0])
 
 
 def shards(
@@ -451,8 +495,8 @@
             pltpu.VMEM((pieces, rows, d_model // pieces), F32),
             pltpu.VMEM((pieces * 16, rows // head_n, d_model // pieces), BF16),
             pltpu.VMEM((pieces * 16, rows // head_n, d_model // pieces), BF16),
-            dma((8,)), dma((pieces * 16,)), dma((pieces * 16,)), dma((2 * heads,)), dma((2 * heads,)),
-            dma(((tok_n + 1) * heads,)), dma(((tok_n + 1) * heads,)), dma((pieces * 16,)), dma((pieces * 16,)),
+            dma((6,)), dma((1,)), dma((AG_SEMS,)), dma((2,)),
+            dma((4,)), dma((4 * heads,)), dma((1,)), dma((RS_SEMS,)),
         ],
         compiler_params=pltpu.CompilerParams(
             collective_id=0, has_side_effects=True, vmem_limit_bytes=60 * 2**20

time: 96.5 us -> 92.6 us (0.960)
  Pallas kernels: 94.7 us -> 90.7 us
    pallas_call x1, Pallas kernels: 94.7 us -> 90.7 us  [shards(): pl.pallas_call(functools.partial(kernel, tok_n), out_shape=jax.ShapeDtype...]
where the time goes in v4:
time: 92.6 us; the launch traced here: 92.4 us
  Pallas kernels  90.7 us (98%)
  local copies, waits for them, and re-layouts  1.67 us (2%)
    pallas_call x1, Pallas kernels, shards(): pl.pallas_call(functools.partial(kernel, tok_n), out_shape=jax.ShapeDtype...  90.7 us

profile of v4, /device:TPU:1, one launch (start us, length us, event | category | flops | bytes accessed | tf_op | source)
XLA Modules:
  0.0 92.4 jit_solution(11426403890845469603)
XLA Ops:
  0.0 90.7 %shard_map.100 = bf16[32,4096]{1,0:T(8,128)(2,1)} custom-call(bf16[512,256]{1,0:T(8,128)(2,1)} %tokens.1, bf16[4096,256]{1,0:T(8,128)(2,1)} %w_query.1, bf16[4096,256]{1,0:T(8,128)(2,1)} %w_key.1, bf16[4096,256]{1,0:T(8,128)(2,1)} %w_value.1, bf16[256,4096]{1,0:T(8,128)(2,1)} %w_out.1, f32[2,128,256]{2,1,0:T(8,128)} %gate.1, f32[2,128,256]{2,1,0:T(8,128)} %upper.1, ...), custom_call_target="tpu_custom_call" | custom-call | tf_op jit(solution)/shard_map/pallas_call | solution.py:473
  90.8 1.7 %copy.12 = bf16[32,4096]{1,0:T(8,128)(2,1)} copy(bf16[32,4096]{1,0:T(8,128)(2,1)} %shard_map.100) | data formatting | bytes 524288

commit v5 on v4

--- a/solution.py
+++ b/solution.py
@@ -133,9 +133,9 @@
 
 
 def kernel(
-    tok_n, tokens, w_query, w_key, w_value, w_out, gate, upper, down, rate, step,
+    tok_n, tokens, w_query, w_key, w_value, w_out, gate, upper, down, rate_in, step_in,
     out,
-    blocks, w_in, w_o, acc, q, kv, g_w, u_w, d_w,
+    blocks, w_in, w_o, acc, q, kv, g_w, u_w, d_w, rate, step,
     grad, pair_in, half, chip_in, grad_sum, att, comb, part, come_in, go_out,
     load_sem, ag_send, ag_recv, halo_sem, ar_send, ar_recv, rs_send, rs_recv,
 ):
@@ -173,6 +173,8 @@
     loads.append(pltpu.make_async_copy(gate, g_w, load_sem.at[2]))
     loads.append(pltpu.make_async_copy(upper, u_w, load_sem.at[3]))
     loads.append(pltpu.make_async_copy(down, d_w, load_sem.at[4]))
+    loads.append(pltpu.make_async_copy(rate_in, rate, load_sem.at[6]))
+    loads.append(pltpu.make_async_copy(step_in, step, load_sem.at[7]))
     loads.append(pltpu.make_async_copy(w_out, w_o, load_sem.at[5]))
     for c in loads:
         c.start()
@@ -283,7 +285,7 @@
             send_sem=halo_sem.at[0], recv_sem=halo_sem.at[1], device_id=tok_at(1), device_id_type=MESH,
         ).start()
 
-    for c in loads[4:7]:
+    for c in loads[4:9]:
         c.wait()
     core = lax.rem(t, 2)
     chip = t // 2
@@ -333,10 +335,6 @@
         grad[i, :, hidden:2 * hidden] = dot(kn, d_up, ((0,), (0,))).astype(BF16)
         grad[i, :, 2 * hidden:] = dot(tg, hid, ((0,), (0,))).astype(BF16)
         pair[i].start()
-    for where, span, j in later:
-        project(where, span, j, j + 1)
-    for i in range(heads):
-        q[i] = acc[0, :, i * head_size:(i + 1) * head_size].astype(BF16)
 
     for i in range(heads):
         pair[i].wait_recv()
@@ -344,6 +342,10 @@
         for k in range(1, chips):
             to = lax.rem(chip + k, chips)
             ar_copy(1, i, half.at[(i,) + cut(to)], chip_in.at[i, k], (to * 2 + core, h)).start()
+    for where, span, j in later:
+        project(where, span, j, j + 1)
+    for i in range(heads):
+        q[i] = acc[0, :, i * head_size:(i + 1) * head_size].astype(BF16)
     mine = cut(chip, core * half_rows)
     for i in range(heads):
         total = half[(i,) + cut(chip)].astype(F32)
@@ -399,7 +401,7 @@
         fast = dot(hid, dw, ((1,), (1,)))
         comb[:, i * head_size:(i + 1) * head_size] = (att[i] + fast).astype(BF16)
 
-    loads[7].wait()
+    loads[9].wait()
     out_rows = out.shape[0]
     piece_cols = out.shape[1] // len(trees)
 
@@ -468,12 +470,11 @@
     pieces = len(MIRRORS)
     any_space = pl.BlockSpec(memory_space=pl.ANY)
     vmem = pl.BlockSpec(memory_space=pltpu.VMEM)
-    smem = pl.BlockSpec(memory_space=pltpu.SMEM)
     dma = pltpu.SemaphoreType.DMA
     return pl.pallas_call(
         functools.partial(kernel, tok_n),
         out_shape=jax.ShapeDtypeStruct((rows // head_n, d_model), BF16),
-        in_specs=[any_space] * 8 + [vmem, smem],
+        in_specs=[any_space] * 10,
         out_specs=vmem,
         scratch_shapes=[
             pltpu.VMEM((head_n, rows, width), BF16),
@@ -485,6 +486,8 @@
             pltpu.VMEM((heads, head_size, hidden), F32),
             pltpu.VMEM((heads, head_size, hidden), F32),
             pltpu.VMEM((heads, hidden, head_size), F32),
+            pltpu.VMEM((heads, rows), F32),
+            pltpu.SMEM((heads,), F32),
             pltpu.VMEM((heads, head_size, 3 * hidden), BF16),
             pltpu.VMEM((heads, head_size // 2, 3 * hidden), BF16),
             pltpu.VMEM((heads, head_size // 2, 3 * hidden), BF16),
@@ -495,7 +498,7 @@
             pltpu.VMEM((pieces, rows, d_model // pieces), F32),
             pltpu.VMEM((pieces * 16, rows // head_n, d_model // pieces), BF16),
             pltpu.VMEM((pieces * 16, rows // head_n, d_model // pieces), BF16),
-            dma((6,)), dma((1,)), dma((AG_SEMS,)), dma((2,)),
+            dma((8,)), dma((1,)), dma((AG_SEMS,)), dma((2,)),
             dma((4,)), dma((4 * heads,)), dma((1,)), dma((RS_SEMS,)),
         ],
         compiler_params=pltpu.CompilerParams(

time: 92.6 us -> 92.2 us (level)
  no operation moved by 1% of the time
where the time goes in v5:
time: 92.2 us; the launch traced here: 92.1 us
  Pallas kernels  90.4 us (98%)
  local copies, waits for them, and re-layouts  1.67 us (2%)
    pallas_call x1, Pallas kernels, shards(): pl.pallas_call(functools.partial(kernel, tok_n), out_shape=jax.ShapeDtype...  90.4 us

profile of v5, /device:TPU:1, one launch (start us, length us, event | category | flops | bytes accessed | tf_op | source)
XLA Modules:
  0.0 92.1 jit_solution(6248545415485464154)
XLA Ops:
  0.0 90.4 %shard_map.100 = bf16[32,4096]{1,0:T(8,128)(2,1)} custom-call(bf16[512,256]{1,0:T(8,128)(2,1)} %tokens.1, bf16[4096,256]{1,0:T(8,128)(2,1)} %w_query.1, bf16[4096,256]{1,0:T(8,128)(2,1)} %w_key.1, bf16[4096,256]{1,0:T(8,128)(2,1)} %w_value.1, bf16[256,4096]{1,0:T(8,128)(2,1)} %w_out.1, f32[2,128,256]{2,1,0:T(8,128)} %gate.1, f32[2,128,256]{2,1,0:T(8,128)} %upper.1, ...), custom_call_target="tpu_custom_call" | custom-call | tf_op jit(solution)/shard_map/pallas_call | solution.py:474
  90.4 1.7 %copy.12 = bf16[32,4096]{1,0:T(8,128)(2,1)} copy(bf16[32,4096]{1,0:T(8,128)(2,1)} %shard_map.100) | data formatting | bytes 524288

commit v6 on v5

--- a/solution.py
+++ b/solution.py
@@ -13,7 +13,7 @@
 SIDE = 4
 RX, RZ, LX, LZ = 43.5e3, 21.7e3, 1.8, 3.5
 AHEAD = 2.0
-PART = 1.2
+PART = 1.5
 LATE = 4.0
 UNIT = 0.25
 AG_SEMS, RS_SEMS = 51, 32

time: 92.2 us -> 92.2 us (level)
  no operation moved by 1% of the time
where the time goes in v6:
time: 92.2 us; the launch traced here: 92.1 us
  Pallas kernels  90.4 us (98%)
  local copies, waits for them, and re-layouts  1.67 us (2%)
    pallas_call x1, Pallas kernels, shards(): pl.pallas_call(functools.partial(kernel, tok_n), out_shape=jax.ShapeDtype...  90.4 us

profile of v6, /device:TPU:1, one launch (start us, length us, event | category | flops | bytes accessed | tf_op | source)
XLA Modules:
  0.0 92.1 jit_solution(6248545415485464154)
XLA Ops:
  0.0 90.4 %shard_map.100 = bf16[32,4096]{1,0:T(8,128)(2,1)} custom-call(bf16[512,256]{1,0:T(8,128)(2,1)} %tokens.1, bf16[4096,256]{1,0:T(8,128)(2,1)} %w_query.1, bf16[4096,256]{1,0:T(8,128)(2,1)} %w_key.1, bf16[4096,256]{1,0:T(8,128)(2,1)} %w_value.1, bf16[256,4096]{1,0:T(8,128)(2,1)} %w_out.1, f32[2,128,256]{2,1,0:T(8,128)} %gate.1, f32[2,128,256]{2,1,0:T(8,128)} %upper.1, ...), custom_call_target="tpu_custom_call" | custom-call | tf_op jit(solution)/shard_map/pallas_call | solution.py:474
  90.4 1.7 %copy.12 = bf16[32,4096]{1,0:T(8,128)(2,1)} copy(bf16[32,4096]{1,0:T(8,128)(2,1)} %shard_map.100) | data formatting | bytes 524288
